TPU v7x, 512 devices: a whole 4x4x16 slice. The times are simulated.
512 devices in a mesh: cluster: 16 (over z), vector: 8 (over y, core), replica: 4 (over x).
Axes of the slice: x: 4, y: 4, z: 16, core: 2. Of those that a mesh axis runs over, the one named last changes fastest.
Arguments:
- samples: bfloat16 [128, 524288], P('vector', ('cluster', 'replica')), may hold values from -6 to 6
- leaf_basis_matrix: bfloat16 [32, 64, 8192], P(None, None, ('cluster', 'replica')), may hold values from -0.75 to 0.75
- transfer: bfloat16 [32, 32, 8192], P(None, None, ('cluster', 'replica')), may hold values from -0.75 to 0.75
- leaf_lists: int32 [4, 8192], P(None, ('cluster', 'replica')), may hold values from 0 to 8191, as said below
- leaf_coupling: bfloat16 [32, 32, 4, 8192], P(None, None, None, ('cluster', 'replica')), may hold values from -0.5 to 0.5
- parent_lists: int32 [4, 4096], P(None, ('cluster', 'replica')), may hold values from 0 to 4095, as said below
- parent_coupling: bfloat16 [32, 32, 4, 4096], P(None, None, None, ('cluster', 'replica')), may hold values from -0.5 to 0.5
- test_matrix: bfloat16 [128, 32], P('vector'), may hold values from -0.5 to 0.5
Outputs:
- product: bfloat16 [128, 524288], P('vector', ('cluster', 'replica'))
- new_basis: float32 [64, 32, 8192], P(None, None, ('cluster', 'replica'))
- fresh_transfer_sketch: float32 [32, 32, 8192], P(None, None, ('cluster', 'replica'))
Inputs may be any that keep to these rules, and one draw needn't show every extreme that they name: `leaf_lists`: every source leaf lies within 128 leaves of its target leaf, and some source lies exactly 128 leaves away. `parent_lists`: every source parent lies within half of 128 parents of its target parent, and some source lies exactly that far away.
All inputs are finite; a program needn't handle non-finite values.
Results may differ from a plain program's by a relative error of at most 0.0062.
Values may be sent and summed in bfloat16 or wider, within the bound.
No kernel may reach another device: no remote copies, remote signals or barrier semaphores. Data moves between devices by JAX's collectives and lax.ppermute only.
A program may use at most 64 MiB of HBM per device.

v0:
```python
import jax
import jax.numpy as jnp
from jax import lax
from jax.sharding import PartitionSpec as P


def extended_2(array, sides, width):
    edges = {}
    for axis, dim in sides:
        peers, length = (lax.axis_size(axis), array.shape[dim])
        up = [(i, (i + 1) % peers) for i in range(peers - 1)]
        last = lax.slice_in_dim(array, length - width, length, axis=dim)
        leading = lax.slice_in_dim(array, 0, width, axis=dim)
        edges[dim] = (
            lax.ppermute(last, axis, up),
            lax.ppermute(leading, axis, [(b, a) for a, b in up]),
        )
    done = []
    for _, dim in sides:
        low, high = edges[dim]
        around = [(width, width) if d in done else (0, 0) for d in range(array.ndim)]
        array = jnp.concatenate([jnp.pad(low, around), array, jnp.pad(high, around)], axis=dim)
        done.append(dim)
    return array


def in_order(parts, dim):
    parts = jnp.moveaxis(parts, 0, dim)
    shape = parts.shape
    return parts.reshape(*shape[:dim], shape[dim] * shape[dim + 1], *shape[dim + 2 :])


def sent_to_all(array, axis):
    peers = lax.axis_size(axis)
    return lax.all_to_all(
        jnp.broadcast_to(array[None], (peers, *array.shape)), axis, 0, 0, tiled=True
    )


def gathered_copies(array, axis, dim):
    return in_order(sent_to_all(array, axis), dim)


def in_one_piece(arrays, axis, dim, along):
    both = jnp.concatenate(arrays, axis=along)
    out, at, finished = (gathered_copies(both, axis, dim), 0, [])
    for a in arrays:
        finished.append(lax.slice_in_dim(out, at, at + a.shape[along], axis=along))
        at += a.shape[along]
    return tuple(finished)


def finish_basis(sketch, width):
    scale = lax.rsqrt(jnp.mean(sketch * sketch, axis=0, keepdims=True) + 1e-06)
    new_basis = sketch * scale
    fresh_transfer_sketch = (
        jnp.einsum("pal,pbl->abl", new_basis, sketch, precision=lax.Precision.HIGHEST) / width
    )
    return (new_basis, fresh_transfer_sketch)


def near_take(extended, lists, count):
    first = lax.axis_index(("cluster", "replica")) * count - count
    local_index = lists - first
    return jnp.take(extended, local_index, axis=2)


def shards(
    samples,
    leaf_basis_matrix,
    transfer,
    leaf_lists,
    leaf_coupling,
    parent_lists,
    parent_coupling,
    test_matrix,
):
    rank, width, leaves = leaf_basis_matrix.shape
    vec_local = samples.shape[0]
    each_leaf_amount = samples.reshape(vec_local, leaves, width)
    leaf_coeff = jnp.einsum(
        "rpl,vlp->rvl", leaf_basis_matrix, each_leaf_amount, preferred_element_type=jnp.float32
    ).astype(jnp.bfloat16)
    pairs = transfer.reshape(rank, rank, leaves // 2, 2)
    children = leaf_coeff.reshape(rank, vec_local, leaves // 2, 2)
    parent_coeff = jnp.einsum(
        "abqc,avqc->bvq", pairs, children, preferred_element_type=jnp.float32
    ).astype(jnp.bfloat16)
    leaf_ext = extended_2(leaf_coeff, ((("cluster", "replica"), 2),), leaves)
    leaf_src = near_take(leaf_ext, leaf_lists, leaves)
    parent_ext = extended_2(parent_coeff, ((("cluster", "replica"), 2),), leaves // 2)
    parent_src = near_take(parent_ext, parent_lists, leaves // 2)
    leaf_far = jnp.einsum(
        "rskt,svkt->rvt", leaf_coupling, leaf_src, preferred_element_type=jnp.float32
    )
    parent_far = jnp.einsum(
        "rskq,svkq->rvq", parent_coupling, parent_src, preferred_element_type=jnp.float32
    )
    descend = jnp.einsum(
        "abqc,bvq->avqc", pairs.astype(jnp.float32), parent_far, precision=lax.Precision.HIGHEST
    )
    leaf_count_total = (leaf_far + descend.reshape(rank, vec_local, leaves)).astype(jnp.bfloat16)
    product = jnp.einsum(
        "etw,ebw->bwt", leaf_basis_matrix, leaf_count_total, preferred_element_type=jnp.float32
    ).astype(jnp.bfloat16)
    moved = lax.all_to_all(product, "vector", split_axis=1, concat_axis=0, tiled=True)
    whole_test = gathered_copies(test_matrix, "vector", 0)
    sketch = jnp.einsum("vlp,vr->prl", moved, whole_test, preferred_element_type=jnp.float32)
    shared_basis_rows, shared_transfer_rows = finish_basis(sketch, width)
    new_basis, fresh_transfer_sketch = in_one_piece(
        (shared_basis_rows, shared_transfer_rows), "vector", 2, 0
    )
    return (product.reshape(vec_local, leaves * width), new_basis, fresh_transfer_sketch)


def solution(mesh):
    placed = (
        P("vector", ("cluster", "replica")),
        P(None, None, ("cluster", "replica")),
        P(None, None, ("cluster", "replica")),
        P(None, ("cluster", "replica")),
        P(None, None, None, ("cluster", "replica")),
        P(None, ("cluster", "replica")),
        P(None, None, None, ("cluster", "replica")),
        P("vector", None),
    )
    return jax.shard_map(
        shards,
        mesh=mesh,
        in_specs=placed,
        out_specs=(
            P("vector", ("cluster", "replica")),
            P(None, None, ("cluster", "replica")),
            P(None, None, ("cluster", "replica")),
        ),
        check_vma=False,
    )
```

profile of v0, /device:TPU:256, one launch (start us, length us, event | category | flops | bytes accessed | tf_op | source)
XLA Modules:
  0.0 124.2 jit_solution(8063657740272689346)
XLA Ops:
  0.6 2.5 %copy.69 = bf16[32,64,128]{1,0,2:T(8,128)(2,1)S(1)} copy(bf16[32,64,128]{2,1,0:T(8,128)(2,1)} %param.9) | data formatting | bytes 1048576 | tf_op args[1]
  3.1 1.5 %reshape.45 = bf16[16,128,64]{2,1,0:T(8,128)(2,1)S(1)} reshape(bf16[16,8192]{1,0:T(8,128)(2,1)} %param.8) | data formatting | bytes 524288 | tf_op jit(solution)/shard_map/reshape | solution.py:80
  4.6 1.4 %copy.71 = bf16[32,32,128]{1,0,2:T(8,128)(2,1)S(1)} copy(bf16[32,32,128]{2,1,0:T(8,128)(2,1)S(1)} %copy-done.3) | data formatting | bytes 524288 | tf_op args[2]
  6.1 0.7 convolution_convert_fusion.1
  7.2 3.4 %collective-permute-start.2 = (bf16[32,16,64]{0,1,2:T(8,128)(2,1)S(1)}, bf16[32,16,64]{0,1,2:T(8,128)(2,1)S(1)}, u32[]{:S(2)}, u32[]{:S(2)}) collective-permute-start(bf16[32,16,64]{0,1,2:T(8,128)(2,1)S(1)} %fusion.18), channel_id=1, source_target_pairs={{0,1},{1,2},{2,3},{3,32},{32,33},{33,34},{34,35},{35,64},{64,65},{... | collective-permute-start | bytes 196616 | tf_op jit(solution)/shard_map/ppermute | solution.py:15
  10.7 5.8 %collective-permute-start.3 = (bf16[32,16,64]{0,1,2:T(8,128)(2,1)S(1)}, bf16[32,16,64]{0,1,2:T(8,128)(2,1)}, u32[]{:S(2)}, u32[]{:S(2)}) collective-permute-start(bf16[32,16,64]{0,1,2:T(8,128)(2,1)S(1)} %fusion.18), channel_id=1, source_target_pairs={{1,0},{2,1},{3,2},{32,3},{33,32},{34,33},{35,34},{64,35},{65,64},{... | collective-permute-start | bytes 196616 | tf_op jit(solution)/shard_map/ppermute | solution.py:16
  16.4 1.9 %collective-permute-start = (bf16[32,16,128]{0,1,2:T(8,128)(2,1)S(1)}, bf16[32,16,128]{0,1,2:T(8,128)(2,1)}, u32[]{:S(2)}, u32[]{:S(2)}) collective-permute-start(bf16[32,16,128]{0,1,2:T(8,128)(2,1)S(1)} %bitcast.94), channel_id=1, source_target_pairs={{0,1},{1,2},{2,3},{3,32},{32,33},{33,34},{34,35},{35,64},{64,65},{... | collective-permute-start | bytes 393224 | tf_op jit(solution)/shard_map/ppermute | solution.py:15
  18.4 7.2 %collective-permute-start.1 = (bf16[32,16,128]{0,1,2:T(8,128)(2,1)S(1)}, bf16[32,16,128]{0,1,2:T(8,128)(2,1)}, u32[]{:S(2)}, u32[]{:S(2)}) collective-permute-start(bf16[32,16,128]{0,1,2:T(8,128)(2,1)S(1)} %bitcast.95), channel_id=1, source_target_pairs={{1,0},{2,1},{3,2},{32,3},{33,32},{34,33},{35,34},{64,35},{65,64},{... | collective-permute-start | bytes 393224 | tf_op jit(solution)/shard_map/ppermute | solution.py:16
  25.6 0.7 reshape.78
  26.3 4.5 %all-to-all-start.1 = ((bf16[8,2,256]{2,1,0:T(2,128)(2,1)}), bf16[8,2,256]{2,1,0:T(2,128)(2,1)S(1)}, u32[]{:S(2)}, u32[]{:S(2)}) async-start(bf16[8,2,256]{2,1,0:T(2,128)(2,1)} %reshape.78), calls=%async_computation.1 | async-start | bytes 16384 | tf_op jit(solution)/shard_map/all_to_all | solution.py:35
  30.9 4.4 %copy.72 = bf16[32,32,4,64]{1,0,3,2:T(8,128)(2,1)} copy(bf16[32,32,4,64]{3,2,1,0:T(4,128)(2,1)} %param.14) | data formatting | bytes 1048576 | tf_op args[6]
  35.4 5.4 %copy.70 = bf16[32,32,4,128]{1,0,3,2:T(8,128)(2,1)} copy(bf16[32,32,4,128]{3,2,1,0:T(4,128)(2,1)} %param.12) | data formatting | bytes 2097152 | tf_op args[4]
  40.8 0.7 copy-done.4
  41.5 1.3 %pad_maximum_fusion.1 = bf16[32,16,192]{0,1,2:T(8,128)(2,1)S(1)} fusion(bf16[32,16,64]{0,1,2:T(8,128)(2,1)} %collective-permute-done.3, bf16[32,16,64]{0,1,2:T(8,128)(2,1)} %copy-done.2, bf16[32,16,64]{0,1,2:T(8,128)(2,1)} %copy-done.4), kind=kLoop, calls=%fused_computation.24 | loop fusion | flops 196608 | bytes 393216 | tf_op jit(solution)/shard_map/concatenate | solution.py:22
  42.8 1.8 %gather_fusion.1 = bf16[256,32,16]{1,2,0:T(8,128)(2,1)} fusion(bf16[32,16,192]{0,1,2:T(8,128)(2,1)S(1)} %pad_maximum_fusion.1, s32[1024]{0:T(1024)S(1)} %pad_clamp_fusion), kind=kCustom, calls=%fused_computation.1 | custom fusion | bytes 525312 | tf_op jit(solution)/shard_map/jit(_take)/gather | solution.py:65
  44.5 2.6 %convolution_bitcast_fusion = f32[32,16,64,1]{0,1,3,2:T(8,128)S(1)} fusion(bf16[32,32,4,64]{1,0,3,2:T(8,128)(2,1)} %copy.72, bf16[4,64,32,16]{2,3,1,0:T(8,128)(2,1)} %bitcast.99, pred[4,64]{1,0:T(4,128)(4,1)S(1)} %get-tuple-element.15), kind=kOutput, calls=%fused_computation.13 | convolution fusion | flops 8519680 | bytes 917760 | tf_op jit(solution)/shard_map/rskq,svkq->rvq/dot_general | solution.py:96
  47.2 5.2 %fusion.31 = f32[64,16,32,2]{2,1,3,0:T(8,128)} fusion(f32[32,16,64,1]{0,1,3,2:T(8,128)S(1)} %convolution_bitcast_fusion, bf16[32,32,64,2]{1,0,3,2:T(8,128)(2,1)S(1)} %bitcast.89), kind=kOutput, calls=%fused_computation.41 | convolution fusion | flops 25165824 | bytes 655360 | tf_op jit(solution)/shard_map/abqc,bvq->avqc/dot_general | solution.py:99
  52.3 2.7 %pad_maximum_fusion = bf16[32,16,384]{0,1,2:T(8,128)(2,1)} fusion(bf16[32,16,128]{0,1,2:T(8,128)(2,1)} %collective-permute-done.1, bf16[32,16,128]{0,1,2:T(8,128)(2,1)S(1)} %bitcast.96, bf16[32,16,128]{0,1,2:T(8,128)(2,1)} %collective-permute-done), kind=kLoop, calls=%fused_computation.6 | loop fusion | flops 393216 | bytes 786432 | tf_op jit(solution)/shard_map/concatenate | solution.py:22
  55.0 3.8 %gather_fusion = bf16[512,32,16]{1,2,0:T(8,128)(2,1)} fusion(bf16[32,16,384]{0,1,2:T(8,128)(2,1)} %pad_maximum_fusion, s32[1024]{0:T(1024)S(1)} %pad_clamp_fusion.1), kind=kCustom, calls=%fused_computation | custom fusion | bytes 1050624 | tf_op jit(solution)/shard_map/jit(_take)/gather | solution.py:65
  58.8 4.0 %fusion.13 = bf16[16,128,64]{2,0,1:T(8,128)(2,1)S(1)} fusion(bf16[32,64,128]{1,0,2:T(8,128)(2,1)S(1)} %copy.69, f32[32,16,128]{0,1,2:T(8,128)} %bitcast.97, bf16[32,32,4,128]{1,0,3,2:T(8,128)(2,1)} %copy.70, bf16[4,128,32,16]{2,3,1,0:T(8,128)(2,1)} %bitcast.98, pred[4,128]{1,0:T(4,128)(4,1)S(1)} %compare_and_fusion.1), kind=kOutput, calls=%fused_computation.12 | convolution fusion | flops 25690112 | bytes 2621952 | tf_op jit(solution)/shard_map/etw,ebw->bwt/dot_general | solution.py:103
  62.8 1.1 reshape.76
  63.9 4.8 %all-to-all-start = ((bf16[8,2,8192]{2,1,0:T(2,128)(2,1)}), bf16[8,2,8192]{2,1,0:T(2,128)(2,1)S(1)}, u32[]{:S(2)}, u32[]{:S(2)}) async-start(bf16[8,2,8192]{2,1,0:T(2,128)(2,1)} %reshape.76), calls=%async_computation | async-start | bytes 524288 | tf_op jit(solution)/shard_map/all_to_all | solution.py:106
  68.8 7.4 %all-to-all-done = bf16[8,2,8192]{2,1,0:T(2,128)(2,1)S(1)} async-done(((bf16[8,2,8192]{2,1,0:T(2,128)(2,1)}), bf16[8,2,8192]{2,1,0:T(2,128)(2,1)S(1)}, u32[]{:S(2)}, u32[]{:S(2)}) %all-to-all-start) | async-done | bytes 262176 | tf_op jit(solution)/shard_map/all_to_all | solution.py:106
  78.0 1.5 %broadcast_in_dim.44 = f32[8,96,32,16]{1,3,2,0:T(8,128)} broadcast(f32[96,32,16]{0,2,1:T(8,128)S(1)} %copy.75), dimensions={1,2,3} | broadcast | bytes 1769472 | tf_op jit(solution)/shard_map/broadcast_in_dim | solution.py:36
  79.5 3.7 %all-to-all-start.2 = ((f32[8,96,32,16]{1,3,2,0:T(8,128)}), f32[8,96,32,16]{1,3,2,0:T(8,128)S(1)}, u32[]{:S(2)}, u32[]{:S(2)}) async-start(f32[8,96,32,16]{1,3,2,0:T(8,128)} %broadcast_in_dim.44), calls=%async_computation.2 | async-start | bytes 4194304 | tf_op jit(solution)/shard_map/all_to_all | solution.py:35
  83.4 1.2 reshape.49
  84.6 25.8 %all-to-all-done.2 = f32[8,96,32,16]{1,3,2,0:T(8,128)S(1)} async-done(((f32[8,96,32,16]{1,3,2,0:T(8,128)}), f32[8,96,32,16]{1,3,2,0:T(8,128)S(1)}, u32[]{:S(2)}, u32[]{:S(2)}) %all-to-all-start.2) | async-done | bytes 1572896 | tf_op jit(solution)/shard_map/all_to_all | solution.py:35
  110.4 2.0 %slice.21 = f32[32,32,8,16]{0,3,1,2:T(8,128)} slice(f32[96,32,8,16]{0,3,1,2:T(8,128)S(1)} %bitcast.86), slice={[64:96], [0:32], [0:8], [0:16]} | slice | bytes 1048576 | tf_op jit(solution)/shard_map/slice | solution.py:48
  112.3 3.9 %copy.77 = f32[32,32,8,16]{1,3,2,0:T(8,128)} copy(f32[32,32,8,16]{0,3,1,2:T(8,128)} %slice.21) | data formatting | bytes 1048576 | tf_op jit(solution)/shard_map/slice | solution.py:48
  116.2 3.0 %copy.79 = f32[32,32,128]{2,1,0:T(8,128)} copy(f32[32,32,128]{1,2,0:T(8,128)} %bitcast.90) | data formatting | bytes 1048576
  119.2 1.6 %copy.76 = f32[64,32,8,16]{0,3,2,1:T(8,128)} copy(f32[64,32,8,16]{0,3,1,2:T(8,128)S(1)} %bitcast.87) | data formatting | bytes 2097152 | tf_op jit(solution)/shard_map/slice | solution.py:48
  120.8 3.4 %copy.78 = f32[64,32,128]{2,1,0:T(8,128)} copy(f32[64,32,128]{0,2,1:T(8,128)} %bitcast.91) | data formatting | bytes 2097152
  (37 shorter events, 2.6 us)
Async XLA Ops:
  0.6 4.0 %copy-start.3 = (bf16[32,32,128]{2,1,0:T(8,128)(2,1)S(1)}, bf16[32,32,128]{2,1,0:T(8,128)(2,1)}, u32[]{:S(2)}) copy-start(bf16[32,32,128]{2,1,0:T(8,128)(2,1)} %param.10) | copy-start | bytes 786436
  6.1 19.5 %copy-start.6 = (bf16[16,32]{1,0:T(8,128)(2,1)S(1)}, bf16[16,32]{1,0:T(8,128)(2,1)}, u32[]{:S(2)}) copy-start(bf16[16,32]{1,0:T(8,128)(2,1)} %param.15) | copy-start | bytes 3076
  6.1 24.7 %copy-start.5 = (s32[4,128]{1,0:T(4,128)S(1)}, s32[4,128]{1,0:T(4,128)}, u32[]{:S(2)}) copy-start(s32[4,128]{1,0:T(4,128)} %param.11) | copy-start | bytes 6148
  6.1 24.7 %copy-start.7 = (s32[4,64]{1,0:T(4,128)S(1)}, s32[4,64]{1,0:T(4,128)}, u32[]{:S(2)}) copy-start(s32[4,64]{1,0:T(4,128)} %param.13) | copy-start | bytes 3076
  7.2 33.5 %copy-start.2 = (bf16[32,16,64]{0,1,2:T(8,128)(2,1)}, bf16[32,16,64]{0,1,2:T(8,128)(2,1)S(1)}, u32[]{:S(2)}) copy-start(bf16[32,16,64]{0,1,2:T(8,128)(2,1)S(1)} %fusion.18) | copy-start | bytes 196612
  7.2 33.5 %collective-permute-start.2 = (bf16[32,16,64]{0,1,2:T(8,128)(2,1)S(1)}, bf16[32,16,64]{0,1,2:T(8,128)(2,1)S(1)}, u32[]{:S(2)}, u32[]{:S(2)}) collective-permute-start(bf16[32,16,64]{0,1,2:T(8,128)(2,1)S(1)} %fusion.18), channel_id=1, source_target_pairs={{0,1},{1,2},{2,3},{3,32},{32,33},{33,34},{34,35},{35,64},{64,65},{... | collective-permute-start | bytes 196616 | tf_op jit(solution)/shard_map/ppermute | solution.py:15
  10.7 30.8 %collective-permute-start.3 = (bf16[32,16,64]{0,1,2:T(8,128)(2,1)S(1)}, bf16[32,16,64]{0,1,2:T(8,128)(2,1)}, u32[]{:S(2)}, u32[]{:S(2)}) collective-permute-start(bf16[32,16,64]{0,1,2:T(8,128)(2,1)S(1)} %fusion.18), channel_id=1, source_target_pairs={{1,0},{2,1},{3,2},{32,3},{33,32},{34,33},{35,34},{64,35},{65,64},{... | collective-permute-start | bytes 196616 | tf_op jit(solution)/shard_map/ppermute | solution.py:16
  16.4 35.9 %collective-permute-start = (bf16[32,16,128]{0,1,2:T(8,128)(2,1)S(1)}, bf16[32,16,128]{0,1,2:T(8,128)(2,1)}, u32[]{:S(2)}, u32[]{:S(2)}) collective-permute-start(bf16[32,16,128]{0,1,2:T(8,128)(2,1)S(1)} %bitcast.94), channel_id=1, source_target_pairs={{0,1},{1,2},{2,3},{3,32},{32,33},{33,34},{34,35},{35,64},{64,65},{... | collective-permute-start | bytes 393224 | tf_op jit(solution)/shard_map/ppermute | solution.py:15
  18.4 34.0 %collective-permute-start.1 = (bf16[32,16,128]{0,1,2:T(8,128)(2,1)S(1)}, bf16[32,16,128]{0,1,2:T(8,128)(2,1)}, u32[]{:S(2)}, u32[]{:S(2)}) collective-permute-start(bf16[32,16,128]{0,1,2:T(8,128)(2,1)S(1)} %bitcast.95), channel_id=1, source_target_pairs={{1,0},{2,1},{3,2},{32,3},{33,32},{34,33},{35,34},{64,35},{65,64},{... | collective-permute-start | bytes 393224 | tf_op jit(solution)/shard_map/ppermute | solution.py:16
  26.3 37.6 %all-to-all-start.1 = ((bf16[8,2,256]{2,1,0:T(2,128)(2,1)}), bf16[8,2,256]{2,1,0:T(2,128)(2,1)S(1)}, u32[]{:S(2)}, u32[]{:S(2)}) async-start(bf16[8,2,256]{2,1,0:T(2,128)(2,1)} %reshape.78), calls=%async_computation.1 | async-start | bytes 16384 | tf_op jit(solution)/shard_map/all_to_all | solution.py:35
  40.8 0.7 copy-start.4
  62.8 14.9 %copy-start = (bf16[16,128,64]{2,0,1:T(8,128)(2,1)}, bf16[16,128,64]{2,0,1:T(8,128)(2,1)S(1)}, u32[]{:S(2)}) copy-start(bf16[16,128,64]{2,0,1:T(8,128)(2,1)S(1)} %fusion.13) | copy-start | bytes 786436
  63.9 12.3 %all-to-all-start = ((bf16[8,2,8192]{2,1,0:T(2,128)(2,1)}), bf16[8,2,8192]{2,1,0:T(2,128)(2,1)S(1)}, u32[]{:S(2)}, u32[]{:S(2)}) async-start(bf16[8,2,8192]{2,1,0:T(2,128)(2,1)} %reshape.76), calls=%async_computation | async-start | bytes 524288 | tf_op jit(solution)/shard_map/all_to_all | solution.py:106
  79.5 3.7 %copy-start.1 = (bf16[16,128,64]{2,0,1:T(8,128)(2,1)S(1)}, bf16[16,128,64]{2,0,1:T(8,128)(2,1)}, u32[]{:S(2)}) copy-start(bf16[16,128,64]{2,0,1:T(8,128)(2,1)} %copy-done) | copy-start | bytes 786436
  79.5 30.8 %all-to-all-start.2 = ((f32[8,96,32,16]{1,3,2,0:T(8,128)}), f32[8,96,32,16]{1,3,2,0:T(8,128)S(1)}, u32[]{:S(2)}, u32[]{:S(2)}) async-start(f32[8,96,32,16]{1,3,2,0:T(8,128)} %broadcast_in_dim.44), calls=%async_computation.2 | async-start | bytes 4194304 | tf_op jit(solution)/shard_map/all_to_all | solution.py:35
where the time goes:
time: 125 us; the launch traced here: 124 us
  local copies, waits for them, and re-layouts  40.6 us (32%)
  waiting for transfers between devices  33.2 us (27%)
  starting transfers between devices  31.3 us (25%)
  matrix products  13.8 us (11%)
  other arithmetic  4.28 us (3%)
    all_to_all x2, waiting for transfers between devices, sent_to_all(): lax.all_to_all(jnp.broadcast_to(array[None], (peers, *array.shape)), axis...  25.8 us
    unnamed x26, local copies, waits for them, and re-layouts  23 us
    ppermute x2, starting transfers between devices, extended_2(): lax.ppermute(leading, axis, [(b, a) for a, b in up])  13 us
    all_to_all x2, starting transfers between devices, sent_to_all(): lax.all_to_all(jnp.broadcast_to(array[None], (peers, *array.shape)), axis...  8.2 us
    slice x3, local copies, waits for them, and re-layouts, in_one_piece(): finished.append(lax.slice_in_dim(out, at, at + a.shape[along], axis=along))  7.48 us
    all_to_all x1, waiting for transfers between devices, shards(): lax.all_to_all(product, 'vector', split_axis=1, concat_axis=0, tiled=True)  7.41 us
    gather x2, local copies, waits for them, and re-layouts, near_take(): return jnp.take(extended, local_index, axis=2)  5.57 us
    ppermute x2, starting transfers between devices, extended_2(): lax.ppermute(last, axis, up)  5.32 us
  transfers between devices with their start and end apart: 7, of which 2 were waited for; matrix products, arithmetic and copies ran while one was open for 28% of the time, Pallas kernels for 0%

commit v1 on v0

--- a/solution.py
+++ b/solution.py
@@ -2,6 +2,13 @@
 import jax.numpy as jnp
 from jax import lax
 from jax.sharding import PartitionSpec as P
+
+
+def swap_blocks(value, axis, split, join):
+    size = lax.axis_size(axis)
+    blocks = jnp.stack(jnp.split(value, size, axis=split), axis=0)
+    blocks = lax.all_to_all(blocks, axis, split_axis=0, concat_axis=0)
+    return jnp.concatenate(blocks, axis=join)
 
 
 def extended_2(array, sides, width):
@@ -103,7 +110,7 @@
     product = jnp.einsum(
         "etw,ebw->bwt", leaf_basis_matrix, leaf_count_total, preferred_element_type=jnp.float32
     ).astype(jnp.bfloat16)
-    moved = lax.all_to_all(product, "vector", split_axis=1, concat_axis=0, tiled=True)
+    moved = swap_blocks(product, "vector", 1, 0)
     whole_test = gathered_copies(test_matrix, "vector", 0)
     sketch = jnp.einsum("vlp,vr->prl", moved, whole_test, preferred_element_type=jnp.float32)
     shared_basis_rows, shared_transfer_rows = finish_basis(sketch, width)

time: 125 us -> 125 us (level)
    unnamed x26 -> x31, local copies, waits for them, and re-layouts: 23 us -> 23.1 us
where the time goes in v1:
time: 125 us; the launch traced here: 124 us
  local copies, waits for them, and re-layouts  40.8 us (33%)
  waiting for transfers between devices  33.2 us (27%)
  starting transfers between devices  31.2 us (25%)
  matrix products  13.6 us (11%)
  other arithmetic  4.37 us (3%)
    all_to_all x2, waiting for transfers between devices, sent_to_all(): lax.all_to_all(jnp.broadcast_to(array[None], (peers, *array.shape)), axis...  25.8 us
    unnamed x31, local copies, waits for them, and re-layouts  23.1 us
    ppermute x2, starting transfers between devices, extended_2(): lax.ppermute(leading, axis, [(b, a) for a, b in up])  13 us
    all_to_all x2, starting transfers between devices, sent_to_all(): lax.all_to_all(jnp.broadcast_to(array[None], (peers, *array.shape)), axis...  8.07 us
    slice x3, local copies, waits for them, and re-layouts, in_one_piece(): finished.append(lax.slice_in_dim(out, at, at + a.shape[along], axis=along))  7.53 us
    all_to_all x1, waiting for transfers between devices, swap_blocks(): blocks = lax.all_to_all(blocks, axis, split_axis=0, concat_axis=0)  7.41 us
    gather x2, local copies, waits for them, and re-layouts, near_take(): return jnp.take(extended, local_index, axis=2)  5.57 us
    ppermute x2, starting transfers between devices, extended_2(): lax.ppermute(last, axis, up)  5.32 us
  transfers between devices with their start and end apart: 7, of which 2 were waited for; matrix products, arithmetic and copies ran while one was open for 28% of the time, Pallas kernels for 0%

profile of v1, /device:TPU:256, one launch (start us, length us, event | category | flops | bytes accessed | tf_op | source)
XLA Modules:
  0.0 124.1 jit_solution(1622782705479816493)
XLA Ops:
  0.6 2.5 %copy.69 = bf16[32,64,128]{1,0,2:T(8,128)(2,1)S(1)} copy(bf16[32,64,128]{2,1,0:T(8,128)(2,1)} %param.9) | data formatting | bytes 1048576 | tf_op args[1]
  3.1 1.5 %reshape.46 = bf16[16,128,64]{2,1,0:T(8,128)(2,1)S(1)} reshape(bf16[16,8192]{1,0:T(8,128)(2,1)} %param.8) | data formatting | bytes 524288 | tf_op jit(solution)/shard_map/reshape | solution.py:87
  4.6 1.4 %copy.71 = bf16[32,32,128]{1,0,2:T(8,128)(2,1)S(1)} copy(bf16[32,32,128]{2,1,0:T(8,128)(2,1)S(1)} %copy-done.2) | data formatting | bytes 524288 | tf_op args[2]
  6.1 0.7 convolution_convert_fusion.1
  7.2 3.4 %collective-permute-start.2 = (bf16[32,16,64]{0,1,2:T(8,128)(2,1)S(1)}, bf16[32,16,64]{0,1,2:T(8,128)(2,1)S(1)}, u32[]{:S(2)}, u32[]{:S(2)}) collective-permute-start(bf16[32,16,64]{0,1,2:T(8,128)(2,1)S(1)} %fusion.18), channel_id=1, source_target_pairs={{0,1},{1,2},{2,3},{3,32},{32,33},{33,34},{34,35},{35,64},{64,65},{... | collective-permute-start | bytes 196616 | tf_op jit(solution)/shard_map/ppermute | solution.py:22
  10.7 5.8 %collective-permute-start.3 = (bf16[32,16,64]{0,1,2:T(8,128)(2,1)S(1)}, bf16[32,16,64]{0,1,2:T(8,128)(2,1)}, u32[]{:S(2)}, u32[]{:S(2)}) collective-permute-start(bf16[32,16,64]{0,1,2:T(8,128)(2,1)S(1)} %fusion.18), channel_id=1, source_target_pairs={{1,0},{2,1},{3,2},{32,3},{33,32},{34,33},{35,34},{64,35},{65,64},{... | collective-permute-start | bytes 196616 | tf_op jit(solution)/shard_map/ppermute | solution.py:23
  16.4 1.9 %collective-permute-start = (bf16[32,16,128]{0,1,2:T(8,128)(2,1)S(1)}, bf16[32,16,128]{0,1,2:T(8,128)(2,1)}, u32[]{:S(2)}, u32[]{:S(2)}) collective-permute-start(bf16[32,16,128]{0,1,2:T(8,128)(2,1)S(1)} %bitcast.123), channel_id=1, source_target_pairs={{0,1},{1,2},{2,3},{3,32},{32,33},{33,34},{34,35},{35,64},{64,65},{... | collective-permute-start | bytes 393224 | tf_op jit(solution)/shard_map/ppermute | solution.py:22
  18.4 7.2 %collective-permute-start.1 = (bf16[32,16,128]{0,1,2:T(8,128)(2,1)S(1)}, bf16[32,16,128]{0,1,2:T(8,128)(2,1)}, u32[]{:S(2)}, u32[]{:S(2)}) collective-permute-start(bf16[32,16,128]{0,1,2:T(8,128)(2,1)S(1)} %bitcast.124), channel_id=1, source_target_pairs={{1,0},{2,1},{3,2},{32,3},{33,32},{34,33},{35,34},{64,35},{65,64},{... | collective-permute-start | bytes 393224 | tf_op jit(solution)/shard_map/ppermute | solution.py:23
  25.6 0.7 reshape.79
  26.3 4.5 %all-to-all-start.1 = ((bf16[8,2,256]{2,1,0:T(2,128)(2,1)}), bf16[8,2,256]{2,1,0:T(2,128)(2,1)S(1)}, u32[]{:S(2)}, u32[]{:S(2)}) async-start(bf16[8,2,256]{2,1,0:T(2,128)(2,1)} %reshape.79), calls=%async_computation.1 | async-start | bytes 16384 | tf_op jit(solution)/shard_map/all_to_all | solution.py:42
  30.9 4.4 %copy.72 = bf16[32,32,4,64]{1,0,3,2:T(8,128)(2,1)} copy(bf16[32,32,4,64]{3,2,1,0:T(4,128)(2,1)} %param.14) | data formatting | bytes 1048576 | tf_op args[6]
  35.3 5.4 %copy.70 = bf16[32,32,4,128]{1,0,3,2:T(8,128)(2,1)} copy(bf16[32,32,4,128]{3,2,1,0:T(4,128)(2,1)} %param.12) | data formatting | bytes 2097152 | tf_op args[4]
  40.8 0.7 copy-done.3
  41.5 1.3 %pad_maximum_fusion.1 = bf16[32,16,192]{0,1,2:T(8,128)(2,1)S(1)} fusion(bf16[32,16,64]{0,1,2:T(8,128)(2,1)} %collective-permute-done.3, bf16[32,16,64]{0,1,2:T(8,128)(2,1)} %copy-done.1, bf16[32,16,64]{0,1,2:T(8,128)(2,1)} %copy-done.3), kind=kLoop, calls=%fused_computation.24 | loop fusion | flops 196608 | bytes 393216 | tf_op jit(solution)/shard_map/concatenate | solution.py:29
  42.8 1.8 %gather_fusion.1 = bf16[256,32,16]{1,2,0:T(8,128)(2,1)} fusion(bf16[32,16,192]{0,1,2:T(8,128)(2,1)S(1)} %pad_maximum_fusion.1, s32[1024]{0:T(1024)S(1)} %pad_clamp_fusion), kind=kCustom, calls=%fused_computation.1 | custom fusion | bytes 525312 | tf_op jit(solution)/shard_map/jit(_take)/gather | solution.py:72
  44.5 2.6 %convolution_bitcast_fusion = f32[32,16,64,1]{0,1,3,2:T(8,128)S(1)} fusion(bf16[32,32,4,64]{1,0,3,2:T(8,128)(2,1)} %copy.72, bf16[4,64,32,16]{2,3,1,0:T(8,128)(2,1)} %bitcast.128, pred[4,64]{1,0:T(4,128)(4,1)S(1)} %get-tuple-element.15), kind=kOutput, calls=%fused_computation.13 | convolution fusion | flops 8519680 | bytes 917760 | tf_op jit(solution)/shard_map/rskq,svkq->rvq/dot_general | solution.py:103
  47.2 5.2 %fusion.40 = f32[64,16,32,2]{2,1,3,0:T(8,128)} fusion(f32[32,16,64,1]{0,1,3,2:T(8,128)S(1)} %convolution_bitcast_fusion, bf16[32,32,64,2]{1,0,3,2:T(8,128)(2,1)S(1)} %bitcast.119), kind=kOutput, calls=%fused_computation.58 | convolution fusion | flops 25165824 | bytes 655360 | tf_op jit(solution)/shard_map/abqc,bvq->avqc/dot_general | solution.py:106
  52.3 2.8 %pad_maximum_fusion = bf16[32,16,384]{0,1,2:T(8,128)(2,1)} fusion(bf16[32,16,128]{0,1,2:T(8,128)(2,1)} %collective-permute-done.1, bf16[32,16,128]{0,1,2:T(8,128)(2,1)S(1)} %bitcast.125, bf16[32,16,128]{0,1,2:T(8,128)(2,1)} %collective-permute-done), kind=kLoop, calls=%fused_computation.6 | loop fusion | flops 393216 | bytes 786432 | tf_op jit(solution)/shard_map/concatenate | solution.py:29
  55.1 3.8 %gather_fusion = bf16[512,32,16]{1,2,0:T(8,128)(2,1)} fusion(bf16[32,16,384]{0,1,2:T(8,128)(2,1)} %pad_maximum_fusion, s32[1024]{0:T(1024)S(1)} %pad_clamp_fusion.1), kind=kCustom, calls=%fused_computation | custom fusion | bytes 1050624 | tf_op jit(solution)/shard_map/jit(_take)/gather | solution.py:72
  58.9 3.8 %fusion.13 = bf16[16,128,64]{2,0,1:T(8,128)(2,1)S(1)} fusion(bf16[32,64,128]{1,0,2:T(8,128)(2,1)S(1)} %copy.69, f32[32,16,128]{0,1,2:T(8,128)S(1)} %bitcast.126, bf16[32,32,4,128]{1,0,3,2:T(8,128)(2,1)} %copy.70, bf16[4,128,32,16]{2,3,1,0:T(8,128)(2,1)} %bitcast.127, pred[4,128]{1,0:T(4,128)(4,1)S(1)} %compare_and_fusion.1), kind=kOutput, calls=%fused_computation.12 | convolution fusion | flops 25690112 | bytes 2621952 | tf_op jit(solution)/shard_map/etw,ebw->bwt/dot_general | solution.py:110
  62.9 1.1 reshape.77
  64.0 4.8 %all-to-all-start = ((bf16[8,2,8192]{2,1,0:T(2,128)(2,1)}), bf16[8,2,8192]{2,1,0:T(2,128)(2,1)S(1)}, u32[]{:S(2)}, u32[]{:S(2)}) async-start(bf16[8,2,8192]{2,1,0:T(2,128)(2,1)} %reshape.77), calls=%async_computation | async-start | bytes 524288 | tf_op jit(solution)/shard_map/all_to_all | solution.py:10
  68.8 7.4 %all-to-all-done = bf16[8,2,8192]{2,1,0:T(2,128)(2,1)S(1)} async-done(((bf16[8,2,8192]{2,1,0:T(2,128)(2,1)}), bf16[8,2,8192]{2,1,0:T(2,128)(2,1)S(1)}, u32[]{:S(2)}, u32[]{:S(2)}) %all-to-all-start) | async-done | bytes 262176 | tf_op jit(solution)/shard_map/all_to_all | solution.py:10
  78.0 1.5 %broadcast_in_dim.44 = f32[8,96,32,16]{1,3,2,0:T(8,128)} broadcast(f32[96,32,16]{0,2,1:T(8,128)S(1)} %copy.75), dimensions={1,2,3} | broadcast | bytes 1769472 | tf_op jit(solution)/shard_map/broadcast_in_dim | solution.py:43
  79.6 3.6 %all-to-all-start.2 = ((f32[8,96,32,16]{1,3,2,0:T(8,128)}), f32[8,96,32,16]{1,3,2,0:T(8,128)S(1)}, u32[]{:S(2)}, u32[]{:S(2)}) async-start(f32[8,96,32,16]{1,3,2,0:T(8,128)} %broadcast_in_dim.44), calls=%async_computation.2 | async-start | bytes 4194304 | tf_op jit(solution)/shard_map/all_to_all | solution.py:42
  83.3 1.2 reshape.50
  84.5 25.8 %all-to-all-done.2 = f32[8,96,32,16]{1,3,2,0:T(8,128)S(1)} async-done(((f32[8,96,32,16]{1,3,2,0:T(8,128)}), f32[8,96,32,16]{1,3,2,0:T(8,128)S(1)}, u32[]{:S(2)}, u32[]{:S(2)}) %all-to-all-start.2) | async-done | bytes 1572896 | tf_op jit(solution)/shard_map/all_to_all | solution.py:42
  110.3 1.9 %slice.21 = f32[32,32,8,16]{0,3,1,2:T(8,128)} slice(f32[96,32,8,16]{0,3,1,2:T(8,128)S(1)} %bitcast.116), slice={[64:96], [0:32], [0:8], [0:16]} | slice | bytes 1048576 | tf_op jit(solution)/shard_map/slice | solution.py:55
  112.2 4.0 %copy.77 = f32[32,32,8,16]{1,3,2,0:T(8,128)} copy(f32[32,32,8,16]{0,3,1,2:T(8,128)} %slice.21) | data formatting | bytes 1048576 | tf_op jit(solution)/shard_map/slice | solution.py:55
  116.2 3.0 %copy.79 = f32[32,32,128]{2,1,0:T(8,128)} copy(f32[32,32,128]{1,2,0:T(8,128)} %bitcast.120) | data formatting | bytes 1048576
  119.1 1.6 %copy.76 = f32[64,32,8,16]{0,3,2,1:T(8,128)} copy(f32[64,32,8,16]{0,3,1,2:T(8,128)S(1)} %bitcast.117) | data formatting | bytes 2097152 | tf_op jit(solution)/shard_map/slice | solution.py:55
  120.7 3.4 %copy.78 = f32[64,32,128]{2,1,0:T(8,128)} copy(f32[64,32,128]{0,2,1:T(8,128)} %bitcast.121) | data formatting | bytes 2097152
  (43 shorter events, 2.7 us)
Async XLA Ops:
  0.6 4.0 %copy-start.2 = (bf16[32,32,128]{2,1,0:T(8,128)(2,1)S(1)}, bf16[32,32,128]{2,1,0:T(8,128)(2,1)}, u32[]{:S(2)}) copy-start(bf16[32,32,128]{2,1,0:T(8,128)(2,1)} %param.10) | copy-start | bytes 786436
  6.1 19.5 %copy-start.5 = (bf16[16,32]{1,0:T(8,128)(2,1)S(1)}, bf16[16,32]{1,0:T(8,128)(2,1)}, u32[]{:S(2)}) copy-start(bf16[16,32]{1,0:T(8,128)(2,1)} %param.15) | copy-start | bytes 3076
  6.1 24.7 %copy-start.4 = (s32[4,128]{1,0:T(4,128)S(1)}, s32[4,128]{1,0:T(4,128)}, u32[]{:S(2)}) copy-start(s32[4,128]{1,0:T(4,128)} %param.11) | copy-start | bytes 6148
  6.1 24.7 %copy-start.6 = (s32[4,64]{1,0:T(4,128)S(1)}, s32[4,64]{1,0:T(4,128)}, u32[]{:S(2)}) copy-start(s32[4,64]{1,0:T(4,128)} %param.13) | copy-start | bytes 3076
  7.2 33.5 %copy-start.1 = (bf16[32,16,64]{0,1,2:T(8,128)(2,1)}, bf16[32,16,64]{0,1,2:T(8,128)(2,1)S(1)}, u32[]{:S(2)}) copy-start(bf16[32,16,64]{0,1,2:T(8,128)(2,1)S(1)} %fusion.18) | copy-start | bytes 196612
  7.2 33.5 %collective-permute-start.2 = (bf16[32,16,64]{0,1,2:T(8,128)(2,1)S(1)}, bf16[32,16,64]{0,1,2:T(8,128)(2,1)S(1)}, u32[]{:S(2)}, u32[]{:S(2)}) collective-permute-start(bf16[32,16,64]{0,1,2:T(8,128)(2,1)S(1)} %fusion.18), channel_id=1, source_target_pairs={{0,1},{1,2},{2,3},{3,32},{32,33},{33,34},{34,35},{35,64},{64,65},{... | collective-permute-start | bytes 196616 | tf_op jit(solution)/shard_map/ppermute | solution.py:22
  10.7 30.8 %collective-permute-start.3 = (bf16[32,16,64]{0,1,2:T(8,128)(2,1)S(1)}, bf16[32,16,64]{0,1,2:T(8,128)(2,1)}, u32[]{:S(2)}, u32[]{:S(2)}) collective-permute-start(bf16[32,16,64]{0,1,2:T(8,128)(2,1)S(1)} %fusion.18), channel_id=1, source_target_pairs={{1,0},{2,1},{3,2},{32,3},{33,32},{34,33},{35,34},{64,35},{65,64},{... | collective-permute-start | bytes 196616 | tf_op jit(solution)/shard_map/ppermute | solution.py:23
  16.4 35.9 %collective-permute-start = (bf16[32,16,128]{0,1,2:T(8,128)(2,1)S(1)}, bf16[32,16,128]{0,1,2:T(8,128)(2,1)}, u32[]{:S(2)}, u32[]{:S(2)}) collective-permute-start(bf16[32,16,128]{0,1,2:T(8,128)(2,1)S(1)} %bitcast.123), channel_id=1, source_target_pairs={{0,1},{1,2},{2,3},{3,32},{32,33},{33,34},{34,35},{35,64},{64,65},{... | collective-permute-start | bytes 393224 | tf_op jit(solution)/shard_map/ppermute | solution.py:22
  18.4 34.0 %collective-permute-start.1 = (bf16[32,16,128]{0,1,2:T(8,128)(2,1)S(1)}, bf16[32,16,128]{0,1,2:T(8,128)(2,1)}, u32[]{:S(2)}, u32[]{:S(2)}) collective-permute-start(bf16[32,16,128]{0,1,2:T(8,128)(2,1)S(1)} %bitcast.124), channel_id=1, source_target_pairs={{1,0},{2,1},{3,2},{32,3},{33,32},{34,33},{35,34},{64,35},{65,64},{... | collective-permute-start | bytes 393224 | tf_op jit(solution)/shard_map/ppermute | solution.py:23
  26.3 37.6 %all-to-all-start.1 = ((bf16[8,2,256]{2,1,0:T(2,128)(2,1)}), bf16[8,2,256]{2,1,0:T(2,128)(2,1)S(1)}, u32[]{:S(2)}, u32[]{:S(2)}) async-start(bf16[8,2,256]{2,1,0:T(2,128)(2,1)} %reshape.79), calls=%async_computation.1 | async-start | bytes 16384 | tf_op jit(solution)/shard_map/all_to_all | solution.py:42
  40.8 0.7 copy-start.3
  52.3 6.6 %copy-start = (f32[64,16,32,2]{2,1,3,0:T(8,128)S(1)}, f32[64,16,32,2]{2,1,3,0:T(8,128)}, u32[]{:S(2)}) copy-start(f32[64,16,32,2]{2,1,3,0:T(8,128)} %fusion.40) | copy-start | bytes 786436
  64.0 12.3 %all-to-all-start = ((bf16[8,2,8192]{2,1,0:T(2,128)(2,1)}), bf16[8,2,8192]{2,1,0:T(2,128)(2,1)S(1)}, u32[]{:S(2)}, u32[]{:S(2)}) async-start(bf16[8,2,8192]{2,1,0:T(2,128)(2,1)} %reshape.77), calls=%async_computation | async-start | bytes 524288 | tf_op jit(solution)/shard_map/all_to_all | solution.py:10
  79.6 30.7 %all-to-all-start.2 = ((f32[8,96,32,16]{1,3,2,0:T(8,128)}), f32[8,96,32,16]{1,3,2,0:T(8,128)S(1)}, u32[]{:S(2)}, u32[]{:S(2)}) async-start(f32[8,96,32,16]{1,3,2,0:T(8,128)} %broadcast_in_dim.44), calls=%async_computation.2 | async-start | bytes 4194304 | tf_op jit(solution)/shard_map/all_to_all | solution.py:42
